TPU v7x, 128 devices: a whole 4x4x4 slice. The times are simulated.
128 devices in a mesh: dp: 8 (over y, core), head: 16 (over z, x).
Axes of the slice: x: 4, y: 4, z: 4, core: 2. Of those that a mesh axis runs over, the one named last changes fastest.
Arguments:
- hidden: bfloat16 [24576, 4096], P('dp'), may hold values from -6 to 6
- weight: bfloat16 [4096, 4096], P('head'), may hold values from -0.09375 to 0.09375
- block_ids: int32 [96, 8], P('dp'), may hold values from 0 to 31, all different within a row
- targets: int32 [24576, 8], P('dp'), may hold values from 0 to 4095
Outputs:
- grad_hidden: bfloat16 [24576, 4096], P('dp', 'head')
- grad_weight: bfloat16 [4096, 4096], P('head', 'dp')
Inputs may be any that keep to these rules, and one draw needn't show every extreme that they name: `block_ids`: each row block lists 8 different label blocks; every label block is listed by some row block. `targets`: a row may repeat a label id.
All inputs are finite; a program needn't handle non-finite values.
Results may differ from a plain program's by a relative error of at most 0.014.
Values may be sent and summed in bfloat16 or wider, within the bound.
A program may use at most 128 MiB of HBM per device.

v0:
```python
import jax
import jax.numpy as jnp
from jax import lax
from jax.sharding import PartitionSpec as P

BLOCK = 128


def local(hidden, weight, block_ids, targets):
    device = lax.axis_index("head")
    owned = weight.shape[0]
    per_device = owned // BLOCK
    row_blocks = block_ids.shape[0]
    block_rows = hidden.shape[0] // row_blocks
    first = device * per_device
    owned_ids = first + jnp.arange(per_device, dtype=jnp.int32)
    logits = jnp.einsum("rd,ld->rl", hidden, weight, preferred_element_type=jnp.float32)
    slot_match = block_ids[:, :, None] == owned_ids[None, None, :]
    listed = jnp.any(slot_match, axis=1)
    row_mask = jnp.broadcast_to(
        listed[:, None, :, None], (row_blocks, block_rows, per_device, BLOCK)
    )
    row_mask = row_mask.reshape(row_blocks * block_rows, owned)
    labels = first * BLOCK + jnp.arange(owned, dtype=jnp.int32)
    hits = jnp.any(targets[:, :, None] == labels[None, None, :], axis=1)
    signal = jax.nn.sigmoid(logits) - hits.astype(jnp.float32)
    grads = jnp.where(row_mask, signal, 0.0).astype(jnp.bfloat16)
    weight_part = jnp.einsum("rl,rd->ld", grads, hidden, preferred_element_type=jnp.float32)
    grad_weight = lax.psum_scatter(
        weight_part.astype(jnp.bfloat16), "dp", scatter_dimension=1, tiled=True
    )
    hidden_part = jnp.dot(grads, weight, preferred_element_type=jnp.float32)
    grad_hidden = lax.psum_scatter(
        hidden_part.astype(jnp.bfloat16), "head", scatter_dimension=1, tiled=True
    )
    return (grad_hidden, grad_weight)


def solution(mesh):
    return jax.shard_map(
        local,
        mesh=mesh,
        in_specs=(P("dp", None), P("head", None), P("dp", None), P("dp", None)),
        out_specs=(P("dp", "head"), P("head", "dp")),
        check_vma=False,
    )
```

profile of v0, /device:TPU:0, one launch (start us, length us, event | category | flops | bytes accessed | tf_op | source)
XLA Modules:
  0.0 256.0 jit_solution(9474276443251819166)
XLA Ops:
  7.2 0.0 copy-start
  7.2 0.0 copy-start.2
  7.2 0.0 reduce-scatter.5.cloned.1.call-start
  7.3 0.9 compare_reduce_fusion.1
  8.2 0.3 broadcast_in_dim.5
  8.5 0.5 copy.13
  9.1 0.9 copy.12
  10.0 0.0 copy-done.2
  10.0 1.6 copy.11
  11.6 18.2 %compare_reduce_fusion = pred[3072,256]{1,0:T(8,128)(4,1)S(1)} fusion(s32[256]{0:T(256)S(1)} %iota_add_fusion, s32[3072,8]{1,0:T(8,128)} %copy.11), kind=kLoop, calls=%fused_computation | loop fusion | flops 11796480 | bytes 885760 | tf_op jit(solution)/shard_map/reduce_or | solution.py:25
  29.8 0.0 copy-done
  29.8 12.5 %fusion.5 = bf16[3072,256]{1,0:T(8,128)(2,1)S(1)} fusion(pred[3072,256]{1,0:T(32,128)(4,1)S(1)} %copy.12, bf16[3072,4096]{1,0:T(8,128)(2,1)} %param.4, bf16[256,4096]{1,0:T(8,128)(2,1)S(1)} %copy-done, pred[3072,256]{1,0:T(8,128)(4,1)S(1)} %compare_reduce_fusion), kind=kOutput, calls=%fused_computation.9 | convolution fusion | flops 6447955968 | bytes 30408704 | tf_op jit(solution)/shard_map/rd,ld->rl/dot_general | solution.py:17
  42.3 0.0 copy-start.1
  42.4 1.1 copy-done.1
  43.5 13.3 %convolution_convert_fusion.1 = bf16[256,4096]{1,0:T(8,128)(2,1)} fusion(bf16[3072,256]{1,0:T(8,128)(2,1)S(1)} %fusion.5, bf16[3072,4096]{1,0:T(8,128)(2,1)} %param.4), kind=kOutput, calls=%fused_computation.2 | convolution fusion | flops 6443499520 | bytes 28835840 | tf_op jit(solution)/shard_map/rl,rd->ld/dot_general | solution.py:28
  56.8 0.0 reduce-scatter.5.cloned.1.call-update
  56.8 0.2 reduce-scatter.3.cloned.1.call-start
  57.0 13.3 %convolution_convert_fusion = bf16[3072,4096]{1,0:T(8,128)(2,1)} fusion(bf16[3072,256]{1,0:T(8,128)(2,1)} %copy-done.1, bf16[256,4096]{1,0:T(8,128)(2,1)S(1)} %copy-done), kind=kOutput, calls=%fused_computation.1 | convolution fusion | flops 6455033856 | bytes 28835840 | tf_op jit(solution)/shard_map/dot_general | solution.py:32
  70.3 0.0 reduce-scatter.3.cloned.1.call-update
  70.4 22.7 %reduce-scatter.5.cloned.1.call-done = bf16[256,512]{1,0:T(8,128)(2,1)} async-done(((bf16[256,4096]{1,0:T(8,128)(2,1)}), bf16[256,512]{1,0:T(8,128)(2,1)}) %reduce-scatter.5.cloned.1.call-update) | async-done | bytes 262160 | tf_op jit(solution)/shard_map/reduce_scatter | solution.py:29
  93.1 156.1 %reduce-scatter.3.cloned.1.call-done = bf16[3072,256]{1,0:T(8,128)(2,1)} async-done(((bf16[3072,4096]{1,0:T(8,128)(2,1)}), bf16[3072,256]{1,0:T(8,128)(2,1)}) %reduce-scatter.3.cloned.1.call-update) | async-done | bytes 1572880 | tf_op jit(solution)/shard_map/reduce_scatter | solution.py:33
  (2 shorter events, 0.0 us)
Async XLA Ops:
  7.2 22.7 %copy-start = (bf16[256,4096]{1,0:T(8,128)(2,1)S(1)}, bf16[256,4096]{1,0:T(8,128)(2,1)}, u32[]{:S(2)}) copy-start(bf16[256,4096]{1,0:T(8,128)(2,1)} %param.5) | copy-start | bytes 6291460
  7.2 2.8 %copy-start.2 = (s32[3072,8]{0,1:T(8,128)S(1)}, s32[3072,8]{0,1:T(8,128)}, u32[]{:S(2)}) copy-start(s32[3072,8]{0,1:T(8,128)} %param.7) | copy-start | bytes 294916
  7.2 85.9 %reduce-scatter.5.cloned.1.call-start = ((), (), s32[]{:S(2)}) async-start(), calls=%async_computation.3 | async-start | bytes 2359296 | tf_op jit(solution)/shard_map/reduce_scatter | solution.py:29
  42.3 1.1 copy-start.1
  56.8 192.4 %reduce-scatter.3.cloned.1.call-start = ((), (), s32[]{:S(2)}) async-start(), calls=%async_computation.2 | async-start | bytes 26738688 | tf_op jit(solution)/shard_map/reduce_scatter | solution.py:33
Sparse Core Ops, SparseCore 0:
  56.9 36.0 reduce-scatter.4
  97.1 152.0 reduce-scatter.2
where the time goes:
time: 257 us; the launch traced here: 256 us
  waiting for transfers between devices  179 us (70%)
  matrix products  39.1 us (15%)
  other arithmetic  19.2 us (7%)
  between operations  14.1 us (5%)
  local copies, waits for them, and re-layouts  4.54 us (2%)
    reduce_scatter x1, waiting for transfers between devices, local(): lax.psum_scatter(hidden_part.astype(jnp.bfloat16), 'head', scatter_dimens...  156 us
    reduce_scatter x1, waiting for transfers between devices, local(): lax.psum_scatter(weight_part.astype(jnp.bfloat16), 'dp', scatter_dimensio...  22.7 us
    reduce_or x1, other arithmetic, local(): hits = jnp.any(targets[:, :, None] == labels[None, None, :], axis=1)  18.2 us
    dot_general x1, matrix products, local(): jnp.einsum('rl,rd->ld', grads, hidden, preferred_element_type=jnp.float32)  13.3 us
    dot_general x1, matrix products, local(): hidden_part = jnp.dot(grads, weight, preferred_element_type=jnp.float32)  13.3 us
    dot_general x1, matrix products, local(): jnp.einsum('rd,ld->rl', hidden, weight, preferred_element_type=jnp.float32)  12.5 us
  transfers between devices with their start and end apart: 2, of which 2 were waited for; matrix products, arithmetic and copies ran while one was open for 5% of the time, Pallas kernels for 0%

commit v1 on v0

v1 whole, which is shorter than its diff:
```python
import functools

import jax
import jax.numpy as jnp
from jax import lax
from jax.experimental import pallas as pl
from jax.experimental.pallas import tpu as pltpu
from jax.sharding import PartitionSpec as P

MESH = pl.DeviceIdType.MESH
BLOCK = 128
F32 = jnp.float32
BF16 = jnp.bfloat16


def kernel(ids_ref, tgt_ref, hid_hbm, w_hbm, gh_hbm, gw_hbm,
           hid, w, wq, g, gt, p, a1, b1, a2, b2, dl, dr, out,
           gwt, gwx, ga1, gb1, ga2, gb2, gdl, gdr, gwo,
           hid_sem, w_sem, out_sem, gwo_sem,
           wz_s, wz_r, wy_s, wy_r, wc_s, wc_r,
           own_s, own_r, fwd_s, fwd_r, hop_s, hop_r, dir_s, dir_r, two_s, two_r,
           gx_s, gx_r, gy_s, gy_r):
    rows = hid.shape[0]
    rb = 256
    half = rb // 2
    n = rows // rb
    dp = lax.axis_index("dp")
    head = lax.axis_index("head")
    y, core = dp // 2, dp % 2
    z, x = head // 4, head % 4

    def up(v, k):
        return lax.rem(v + k, 4)

    zR, zL, zO = up(z, 1), up(z, 3), up(z, 2)
    xR, xL, xO = up(x, 1), up(x, 3), up(x, 2)
    yR, yL, yO = up(y, 1), up(y, 3), up(y, 2)

    def at_z(zz):
        return (dp, zz * 4 + x)

    def at_x(xx):
        return (dp, z * 4 + xx)

    def at_y(yy):
        return (yy * 2 + core, head)

    sibling = (y * 2 + 1 - core, head)

    def remote(src, dst, ss, rs, dev):
        return pltpu.make_async_remote_copy(
            src_ref=src, dst_ref=dst, send_sem=ss, recv_sem=rs, device_id=dev, device_id_type=MESH)

    def chunk(c):
        return pl.ds(pl.multiple_of(c * rb, rb), rb)

    def half_a(c):
        return pl.ds(pl.multiple_of(c * rb, rb), half)

    def half_b(c):
        return pl.ds(pl.multiple_of(c * rb + half, half), half)

    def load_hid(c):
        return pltpu.make_async_copy(hid_hbm.at[chunk(c)], hid.at[chunk(c)], hid_sem.at[c])

    load_w = pltpu.make_async_copy(w_hbm, w, w_sem.at[0])
    load_wq = pltpu.make_async_copy(
        w_hbm.at[:, pl.ds(pl.multiple_of(z * 1024, 1024), 1024)], wq.at[0], w_sem.at[1])

    load_w.start()
    load_hid(0).start()
    load_hid(1).start()
    load_wq.start()

    @pl.loop(2, n)
    def _(c):
        load_hid(c).start()

    barrier = pltpu.get_barrier_semaphore()
    for dev in (at_z(zR), at_z(zL), at_z(zO), at_x(xR), at_x(xL), at_y(yR), at_y(yL), at_y(yO), sibling):
        pl.semaphore_signal(barrier, inc=1, device_id=dev, device_id_type=MESH)
    pl.semaphore_wait(barrier, 9)

    piece = 32
    mine = pl.ds(pl.multiple_of(dp * piece, piece), piece)

    def wz(k):
        to = (zR, zL, zO)[k]
        return remote(w_hbm.at[mine, pl.ds(pl.multiple_of(to * 1024, 1024), 1024)],
                      wq.at[k + 1, mine], wz_s.at[k], wz_r.at[k], at_z(to))

    def wy(k):
        to = (yR, yL, yO)[k]
        return remote(wq.at[pl.ds(1, 3), mine], wq.at[pl.ds(1, 3), mine], wy_s.at[k], wy_r.at[k], at_y(to))

    def wc(k):
        frm = ((y, yL, yR, yO)[k]) * 2 + core
        part = pl.ds(pl.multiple_of(frm * piece, piece), piece)
        return remote(wq.at[pl.ds(1, 3), part], wq.at[pl.ds(1, 3), part], wc_s.at[k], wc_r.at[k], sibling)

    for k in range(3):
        wz(k).start()

    def own_R(c):
        return remote(g.at[0, chunk(c)], g.at[1, chunk(c)], own_s.at[0, c], own_r.at[0, c], at_z(zR))

    def own_L(c):
        return remote(g.at[0, chunk(c)], g.at[2, chunk(c)], own_s.at[1, c], own_r.at[1, c], at_z(zL))

    def fwd_R(c):
        return remote(g.at[1, half_a(c)], g.at[3, half_a(c)], fwd_s.at[0, c], fwd_r.at[0, c], at_z(zR))

    def fwd_L(c):
        return remote(g.at[2, half_b(c)], g.at[3, half_b(c)], fwd_s.at[1, c], fwd_r.at[1, c], at_z(zL))

    def hop_R(c):
        return remote(p.at[xO, half_a(c)], a1.at[c], hop_s.at[0, c], hop_r.at[0, c], at_x(xR))

    def hop_L(c):
        return remote(p.at[xO, half_b(c)], b1.at[c], hop_s.at[1, c], hop_r.at[1, c], at_x(xL))

    def dir_R(c):
        return remote(p.at[xR, half_b(c)], dl.at[c], dir_s.at[0, c], dir_r.at[0, c], at_x(xR))

    def dir_L(c):
        return remote(p.at[xL, half_a(c)], dr.at[c], dir_s.at[1, c], dir_r.at[1, c], at_x(xL))

    def two_R(c):
        return remote(a1.at[c], a2.at[c], two_s.at[0, c], two_r.at[0, c], at_x(xR))

    def two_L(c):
        return remote(b1.at[c], b2.at[c], two_s.at[1, c], two_r.at[1, c], at_x(xL))

    def store_out(c):
        return pltpu.make_async_copy(out.at[chunk(c)], gh_hbm.at[chunk(c)], out_sem.at[c])

    first = head * 2
    labels = first * BLOCK + lax.broadcasted_iota(jnp.int32, (256, rb), 0)

    def signal(c):
        load_hid(c).wait()
        t = lax.dot_general(w[...], hid[chunk(c), :], (((1,), (1,)), ((), ())), preferred_element_type=F32)
        lo = jnp.int32(0)
        hi = jnp.int32(0)
        for k in range(ids_ref.shape[0]):
            ident = ids_ref[k, c]
            lo = lo + (ident == first).astype(jnp.int32)
            hi = hi + (ident == first + 1).astype(jnp.int32)
        tg = tgt_ref[:, chunk(c)]
        hits = labels == tg[0:1, :]
        for k in range(1, tgt_ref.shape[0]):
            hits = hits | (labels == tg[k:k + 1, :])
        s = jax.nn.sigmoid(t) - hits.astype(F32)
        block = lax.broadcasted_iota(jnp.int32, (256, rb), 0) // BLOCK
        on = jnp.where(block == 0, lo, hi) > 0
        s = jnp.where(on, s, 0.0)
        gt[:, chunk(c)] = s.astype(BF16)
        g[0, chunk(c), :] = s.T.astype(BF16)

    def gw_tile(j):
        cols = pl.ds(pl.multiple_of(j * 512, 512), 512)
        t = jnp.dot(gt[...], hid[:, cols], preferred_element_type=F32)
        gwt[j] = t.astype(BF16)

    def gx(k):
        return remote(gwt.at[2 * k + 1 - core], gwx.at[k], gx_s.at[k], gx_r.at[k], sibling)

    A, B = pl.ds(0, 128), pl.ds(128, 128)

    def gy(k):
        src, dst, to = (
            (gwx.at[yO, A], ga1, yR), (gwx.at[yO, B], gb1, yL),
            (gwx.at[yR, B], gdl, yR), (gwx.at[yL, A], gdr, yL),
            (ga1, ga2, yR), (gb1, gb2, yL))[k]
        return remote(src, dst, gy_s.at[k], gy_r.at[k], at_y(to))

    store_gw = pltpu.make_async_copy(gwo, gw_hbm, gwo_sem.at[0])

    load_w.wait()
    signal(0)
    load_wq.wait()
    for k in range(3):
        wz(k).wait_recv()
    for k in range(3):
        wy(k).start()
    wc(0).start()

    @pl.loop(0, n + 4)
    def _(s):
        @pl.when((s >= 1) & (s < n + 1))
        def _():
            own_R(s - 1).wait_recv()
            own_L(s - 1).wait_recv()
            fwd_R(s - 1).start()
            fwd_L(s - 1).start()

        @pl.when(s < n)
        def _():
            own_R(s).start()
            own_L(s).start()

        @pl.when(s == 1)
        def _():
            for k in range(3):
                wy(k).wait_recv()
            for k in range(1, 4):
                wc(k).start()

        @pl.when(s == 2)
        def _():
            for k in range(4):
                wc(k).wait_recv()

        @pl.when((s >= 2) & (s < n + 2))
        def _():
            c = s - 2
            fwd_R(c).wait_recv()
            fwd_L(c).wait_recv()
            lhs = jnp.concatenate([g[k, chunk(c), :] for k in range(4)], axis=1)
            rhs = wq[...].reshape(1024, 1024)
            part = jnp.dot(lhs, rhs, preferred_element_type=F32).astype(BF16)
            for k in range(4):
                p[k, chunk(c), :] = part[:, k * 256:(k + 1) * 256]
            hop_R(c).start()
            hop_L(c).start()
            dir_R(c).start()
            dir_L(c).start()

        @pl.when((s >= 3) & (s < n + 3))
        def _():
            c = s - 3
            hop_R(c).wait_recv()
            a1[c] = (a1[c].astype(F32) + p[xR, half_a(c), :].astype(F32)).astype(BF16)
            two_R(c).start()
            hop_L(c).wait_recv()
            b1[c] = (b1[c].astype(F32) + p[xL, half_b(c), :].astype(F32)).astype(BF16)
            two_L(c).start()

        @pl.when(s >= 4)
        def _():
            c = s - 4
            dir_L(c).wait_recv()
            two_R(c).wait_recv()
            out[half_a(c), :] = (p[x, half_a(c), :].astype(F32) + a2[c].astype(F32) + dr[c].astype(F32)).astype(BF16)
            dir_R(c).wait_recv()
            two_L(c).wait_recv()
            out[half_b(c), :] = (p[x, half_b(c), :].astype(F32) + b2[c].astype(F32) + dl[c].astype(F32)).astype(BF16)
            store_out(c).start()
            for copy in (own_R, own_L, fwd_R, fwd_L, hop_R, hop_L, dir_R, dir_L, two_R, two_L):
                copy(c).wait_send()

        @pl.when(s < 6)
        def _():
            signal(2 * s + 1)

        @pl.when(s < 5)
        def _():
            signal(2 * s + 2)

        @pl.when((s >= 6) & (s < 10))
        def _():
            for k in range(2):
                i = 2 * (s - 6) + k
                gw_tile(2 * lax.rem(i, 4) + jnp.where(i < 4, 1 - core, core))

        @pl.when((s == 6) | (s == 7))
        def _():
            gx(2 * (s - 6)).start()
            gx(2 * (s - 6) + 1).start()

        @pl.when(s == 10)
        def _():
            for k in range(4):
                gx(k).wait_recv()
                gwx[k] = (gwx[k].astype(F32) + gwt[2 * k + core].astype(F32)).astype(BF16)
            for k in range(4):
                gy(k).start()

        @pl.when(s == 11)
        def _():
            gy(0).wait_recv()
            ga1[...] = (ga1[...].astype(F32) + gwx[yR, A, :].astype(F32)).astype(BF16)
            gy(4).start()
            gy(1).wait_recv()
            gb1[...] = (gb1[...].astype(F32) + gwx[yL, B, :].astype(F32)).astype(BF16)
            gy(5).start()

        @pl.when(s == 13)
        def _():
            gy(3).wait_recv()
            gy(4).wait_recv()
            gwo[A, :] = (gwx[y, A, :].astype(F32) + ga2[...].astype(F32) + gdr[...].astype(F32)).astype(BF16)
            gy(2).wait_recv()
            gy(5).wait_recv()
            gwo[B, :] = (gwx[y, B, :].astype(F32) + gb2[...].astype(F32) + gdl[...].astype(F32)).astype(BF16)
            store_gw.start()

    for k in range(3):
        wz(k).wait_send()
        wy(k).wait_send()
    for k in range(4):
        wc(k).wait_send()
        gx(k).wait_send()
    for k in range(6):
        gy(k).wait_send()

    @pl.loop(0, n)
    def _(c):
        store_out(c).wait()
    store_gw.wait()


def local(hidden, weight, block_ids, targets):
    rows, width = hidden.shape
    owned = weight.shape[0]
    n = rows // 256
    dma = pltpu.SemaphoreType.DMA
    v = lambda *shape: pltpu.VMEM(shape, BF16)
    scratch = [
        v(rows, width), v(owned, width), v(4, owned, 1024), v(4, rows, owned), v(owned, rows), v(4, rows, 256),
        v(n, 128, 256), v(n, 128, 256), v(n, 128, 256), v(n, 128, 256), v(n, 128, 256), v(n, 128, 256),
        v(rows, 256),
        v(8, owned, 512), v(4, owned, 512),
        v(128, 512), v(128, 512), v(128, 512), v(128, 512), v(128, 512), v(128, 512), v(owned, 512),
        dma((n,)), dma((2,)), dma((n,)), dma((1,)),
        dma((3,)), dma((3,)), dma((3,)), dma((3,)), dma((4,)), dma((4,)),
    ] + [dma((2, n))] * 10 + [dma((4,)), dma((4,)), dma((6,)), dma((6,))]
    anywhere = pl.BlockSpec(memory_space=pl.ANY)
    return pl.pallas_call(
        kernel,
        out_shape=(jax.ShapeDtypeStruct((rows, 256), BF16), jax.ShapeDtypeStruct((owned, 512), BF16)),
        in_specs=[pl.BlockSpec(memory_space=pltpu.SMEM), pl.BlockSpec(memory_space=pltpu.VMEM), anywhere, anywhere],
        out_specs=(anywhere, anywhere),
        scratch_shapes=scratch,
        compiler_params=pltpu.CompilerParams(
            collective_id=0, has_side_effects=True, vmem_limit_bytes=60 * 1024 * 1024),
        cost_estimate=pl.CostEstimate(flops=3 * 2 * rows * owned * width, bytes_accessed=2 * rows * width, transcendentals=rows * owned),
    )(block_ids.T, targets.T, hidden, weight)


def solution(mesh):
    return jax.shard_map(
        local,
        mesh=mesh,
        in_specs=(P("dp", None), P("head", None), P("dp", None), P("dp", None)),
        out_specs=(P("dp", "head"), P("head", "dp")),
        check_vma=False,
    )
```

time: 257 us -> 106 us (0.41)
  waiting for transfers between devices: 179 us -> 0 us
  Pallas kernels: 0 us -> 101 us
  matrix products: 39.1 us -> 0 us
  other arithmetic: 19.2 us -> 0 us
  between operations: 14.1 us -> 0.65 us
    reduce_scatter x2 -> x0, waiting for transfers between devices: 179 us -> none  [the longest x1 156 us: local(): lax.psum_scatter(hidden_part.astype(jnp.bfloat16), 'head', scatter_dimens...]
    pallas_call x0 -> x1, Pallas kernels: none -> 101 us  [local(): pl.pallas_call(kernel, out_shape=(jax.ShapeDtypeStruct((rows, 256), BF16)...]
    dot_general x3 -> x0, matrix products: 39.1 us -> none  [the longest x1 13.3 us: local(): jnp.einsum('rl,rd->ld', grads, hidden, preferred_element_type=jnp.float32)]
    reduce_or x2 -> x0, other arithmetic: 19.1 us -> none  [the longest x1 18.2 us: local(): hits = jnp.any(targets[:, :, None] == labels[None, None, :], axis=1)]
  transfers between devices with their start and end apart: 2 -> 0, of which waited for: 2 -> 0; matrix products, arithmetic and copies ran while one was open for 5% -> 0% of each run, Pallas kernels for 0% -> 0%
where the time goes in v1:
time: 106 us; the launch traced here: 105 us
  Pallas kernels  101 us (95%)
  local copies, waits for them, and re-layouts  3.4 us (3%)
    pallas_call x1, Pallas kernels, local(): pl.pallas_call(kernel, out_shape=(jax.ShapeDtypeStruct((rows, 256), BF16)...  101 us
    unnamed x4, local copies, waits for them, and re-layouts  3.4 us

profile of v1, /device:TPU:0, one launch (start us, length us, event | category | flops | bytes accessed | tf_op | source)
XLA Modules:
  0.0 105.2 jit_solution(3387680002607008567)
XLA Ops:
  0.6 101.2 %shard_map.59 = (bf16[3072,256]{1,0:T(8,128)(2,1)}, bf16[256,512]{1,0:T(8,128)(2,1)}) custom-call(s32[8,12]{1,0:T(8,128)} %bitcast.3, s32[8,3072]{1,0:T(8,128)} %bitcast.2, bf16[3072,4096]{1,0:T(8,128)(2,1)} %hid_hbm.1, bf16[256,4096]{1,0:T(8,128)(2,1)} %w_hbm.1), custom_call_target="tpu_custom_call" | custom-call | flops 19327352832 | bytes 25165824 | tf_op jit(solution)/shard_map/pallas_call | solution.py:329
  101.8 0.0 copy-start
  101.8 2.7 %copy.8 = bf16[3072,256]{1,0:T(8,128)(2,1)} copy(bf16[3072,256]{1,0:T(8,128)(2,1)} %get-tuple-element.4) | data formatting | bytes 3145728
  104.5 0.0 copy-done
  104.5 0.7 copy.9
Async XLA Ops:
  101.8 2.7 %copy-start = (bf16[256,512]{1,0:T(8,128)(2,1)S(1)}, bf16[256,512]{1,0:T(8,128)(2,1)}, u32[]{:S(2)}) copy-start(bf16[256,512]{1,0:T(8,128)(2,1)} %get-tuple-element.5) | copy-start | bytes 786436

commit v2 on v0

v2 whole, which is shorter than its diff:
```python
import jax
import jax.numpy as jnp
from jax import lax
from jax.experimental import pallas as pl
from jax.experimental.pallas import tpu as pltpu
from jax.sharding import PartitionSpec as P

MESH = pl.DeviceIdType.MESH
BLOCK = 128
F32 = jnp.float32
BF16 = jnp.bfloat16
RL = 256
RB = 128


def kernel(ids_ref, tgt_ref, hid_hbm, w_hbm, gh_hbm, gw_hbm,
           hid, w, wq, g, gt, p, a1, b1, a2, b2, dl, dr, out,
           gwt, gwx, ga1, gb1, ga2, gb2, gdl, gdr, gwo,
           hid_sem, w_sem, out_sem, gwo_sem,
           wz_s, wz_r, wx_s, wx_r, wy_s, wy_r, wc_s, wc_r,
           own_s, own_r, fwd_s, fwd_r, hop_s, hop_r, dir_s, dir_r, two_s, two_r,
           gx_s, gx_r, gy_s, gy_r):
    rows = hid.shape[0]
    half = RB // 2
    nb = rows // RL
    nc = rows // RB
    dp = lax.axis_index("dp")
    head = lax.axis_index("head")
    y, core = dp // 2, dp % 2
    z, x = head // 4, head % 4

    def ring(v):
        return lax.rem(v + 1, 4), lax.rem(v + 3, 4), lax.rem(v + 2, 4)

    zs, xs, ys = ring(z), ring(x), ring(y)
    to_z = [(dp, v * 4 + x) for v in zs]
    to_x = [(dp, z * 4 + v) for v in xs]
    to_y = [(v * 2 + core, head) for v in ys]
    gather_to = (to_z, to_x)
    reduce_to = (to_x, to_z)
    reduce_at = (xs, zs)
    reduce_me = (x, z)
    sibling = (y * 2 + 1 - core, head)

    def remote(src, dst, ss, rs, dev):
        return pltpu.make_async_remote_copy(
            src_ref=src, dst_ref=dst, send_sem=ss, recv_sem=rs, device_id=dev, device_id_type=MESH)

    def span(start, size):
        return pl.ds(pl.multiple_of(start, size), size)

    def block(b):
        return span(b * RL, RL)

    def low(b):
        return span(b * RL, RL // 2)

    def high(b):
        return span(b * RL + RL // 2, RL // 2)

    def half_a(c):
        return span(c * RB, half)

    def half_b(c):
        return span(c * RB + half, half)

    def load_hid(b):
        return pltpu.make_async_copy(hid_hbm.at[block(b)], hid.at[block(b)], hid_sem.at[b])

    load_w = pltpu.make_async_copy(w_hbm, w, w_sem.at[0])
    load_wz = pltpu.make_async_copy(w_hbm.at[:, span(z * 1024, 1024)], wq.at[0, 0], w_sem.at[1])

    def load_wx(k):
        return pltpu.make_async_copy(
            w_hbm.at[:, span((k * 4 + x) * 256, 256)], wq.at[1, 0, :, pl.ds(k * 256, 256)], w_sem.at[2 + k])

    load_w.start()
    load_hid(0).start()
    load_hid(nb // 2).start()

    @pl.loop(1, nb // 2)
    def _(b):
        load_hid(b).start()
        load_hid(b + nb // 2).start()

    load_wz.start()
    for k in range(4):
        load_wx(k).start()

    barrier = pltpu.get_barrier_semaphore()
    peers = to_z + to_x + to_y + [sibling]
    for dev in peers:
        pl.semaphore_signal(barrier, inc=1, device_id=dev, device_id_type=MESH)
    pl.semaphore_wait(barrier, len(peers))

    piece = w.shape[0] // 8
    mine = span(dp * piece, piece)

    def wz(k):
        return remote(w_hbm.at[mine, span(zs[k] * 1024, 1024)], wq.at[0, k + 1, mine],
                      wz_s.at[k], wz_r.at[k], to_z[k])

    def wx(k, j):
        return remote(w_hbm.at[mine, span((j * 4 + xs[k]) * 256, 256)], wq.at[1, k + 1, mine, pl.ds(j * 256, 256)],
                      wx_s.at[k, j], wx_r.at[k, j], to_x[k])

    def wy(o, k):
        part = wq.at[o, pl.ds(1, 3), mine]
        return remote(part, part, wy_s.at[o, k], wy_r.at[o, k], to_y[k])

    def wc(o, k):
        frm = (y, ys[1], ys[0], ys[2])[k] * 2 + core
        part = wq.at[o, pl.ds(1, 3), span(frm * piece, piece)]
        return remote(part, part, wc_s.at[o, k], wc_r.at[o, k], sibling)

    for k in range(3):
        wz(k).start()
        for j in range(4):
            wx(k, j).start()

    def own(o, k, b):
        return remote(g.at[0, block(b)], g.at[k + 1, block(b)], own_s.at[k, b], own_r.at[k, b], gather_to[o][k])

    def fwd(o, k, b):
        part = (low, high)[k](b)
        return remote(g.at[k + 1, part], g.at[3, part], fwd_s.at[k, b], fwd_r.at[k, b], gather_to[o][k])

    def hop(o, k, c):
        part, dst = ((half_a(c), a1), (half_b(c), b1))[k]
        return remote(p.at[reduce_at[o][2], part], dst.at[c], hop_s.at[k, c], hop_r.at[k, c], reduce_to[o][k])

    def direct(o, k, c):
        part, dst = ((half_b(c), dl), (half_a(c), dr))[k]
        return remote(p.at[reduce_at[o][k], part], dst.at[c], dir_s.at[k, c], dir_r.at[k, c], reduce_to[o][k])

    def two(o, k, c):
        src, dst = ((a1, a2), (b1, b2))[k]
        return remote(src.at[c], dst.at[c], two_s.at[k, c], two_r.at[k, c], reduce_to[o][k])

    def store_out(c):
        return pltpu.make_async_copy(out.at[span(c * RB, RB)], gh_hbm.at[span(c * RB, RB)], out_sem.at[c])

    first = head * 2
    labels = first * BLOCK + lax.broadcasted_iota(jnp.int32, (2 * BLOCK, RL), 0)
    upper = lax.broadcasted_iota(jnp.int32, (2 * BLOCK, RL), 0) >= BLOCK

    def signal(b):
        load_hid(b).wait()
        t = lax.dot_general(w[...], hid[block(b), :], (((1,), (1,)), ((), ())), preferred_element_type=F32)
        lo = jnp.int32(0)
        hi = jnp.int32(0)
        for k in range(ids_ref.shape[0]):
            ident = ids_ref[k, b]
            lo = lo + (ident == first).astype(jnp.int32)
            hi = hi + (ident == first + 1).astype(jnp.int32)
        tg = tgt_ref[:, block(b)]
        hits = labels == tg[0:1, :]
        for k in range(1, tgt_ref.shape[0]):
            hits = hits | (labels == tg[k:k + 1, :])
        s = jax.nn.sigmoid(t) - hits.astype(F32)
        s = jnp.where(jnp.where(upper, hi, lo) > 0, s, 0.0)
        gt[:, block(b)] = s.astype(BF16)
        g[0, block(b), :] = s.T.astype(BF16)

    def gw_tile(j):
        t = jnp.dot(gt[...], hid[:, span(j * 512, 512)], preferred_element_type=F32)
        gwt[j] = t.astype(BF16)

    def gx(k):
        return remote(gwt.at[2 * k + 1 - core], gwx.at[k], gx_s.at[k], gx_r.at[k], sibling)

    A, B = pl.ds(0, 128), pl.ds(128, 128)

    def gy(k):
        src, dst, to = (
            (gwx.at[ys[2], A], ga1, 0), (gwx.at[ys[2], B], gb1, 1),
            (gwx.at[ys[0], B], gdl, 0), (gwx.at[ys[1], A], gdr, 1),
            (ga1, ga2, 0), (gb1, gb2, 1))[k]
        return remote(src, dst, gy_s.at[k], gy_r.at[k], to_y[to])

    store_gw = pltpu.make_async_copy(gwo, gw_hbm, gwo_sem.at[0])

    def add(*parts):
        total = parts[0].astype(F32)
        for part in parts[1:]:
            total = total + part.astype(F32)
        return total.astype(BF16)

    load_w.wait()

    nh = nb // 2
    LA = 2

    @pl.loop(0, nh + 4)
    def _(s):
        for o in range(2):
            @pl.when(s < nh)
            def _():
                b = s + o * nh
                signal(b)
                for k in range(2):
                    own(o, k, b).start()

            @pl.when((s >= LA) & (s < nh + LA))
            def _():
                b = s - LA + o * nh
                for k in range(2):
                    own(o, k, b).wait_recv()
                    fwd(o, k, b).start()

        @pl.when(s == 1)
        def _():
            load_wz.wait()
            for k in range(4):
                load_wx(k).wait()
            for k in range(3):
                wz(k).wait_recv()
                for j in range(4):
                    wx(k, j).wait_recv()
            for o in range(2):
                for k in range(3):
                    wy(o, k).start()
                wc(o, 0).start()

        @pl.when(s == 7)
        def _():
            for o in range(2):
                for k in range(3):
                    wy(o, k).wait_recv()
                    wc(o, k + 1).start()

        @pl.when(s >= nh)
        def _():
            for k in range(2):
                i = 2 * (s - nh) + k
                gw_tile(2 * lax.rem(i, 4) + jnp.where(i < 4, 1 - core, core))

        @pl.when((s >= nh) & (s < nh + 2))
        def _():
            for k in range(2):
                gx(2 * (s - nh) + k).start()

    for o in range(2):
        for k in range(4):
            wc(o, k).wait_recv()

    mh = nc // 2
    LD = 2
    LE = 4

    @pl.loop(0, mh + LE)
    def _(s):
        @pl.when(s < mh)
        def _():
            @pl.when(s % 2 == 0)
            def _():
                for o in range(2):
                    for k in range(2):
                        fwd(o, k, s // 2 + o * nh).wait_recv()

            for o in range(2):
                c = s + o * mh
                lhs = jnp.concatenate([g[k, span(c * RB, RB), :] for k in range(4)], axis=1)
                part = jnp.dot(lhs, wq[o].reshape(1024, 1024), preferred_element_type=F32).astype(BF16)
                for k in range(4):
                    p[k, span(c * RB, RB), :] = part[:, k * 256:(k + 1) * 256]
                for k in range(2):
                    hop(o, k, c).start()
                for k in range(2):
                    direct(o, k, c).start()

        @pl.when((s >= LD) & (s < mh + LD))
        def _():
            for o in range(2):
                c = s - LD + o * mh
                right, left, _ = reduce_at[o]
                hop(o, 0, c).wait_recv()
                a1[c] = add(a1[c], p[right, half_a(c), :])
                two(o, 0, c).start()
                hop(o, 1, c).wait_recv()
                b1[c] = add(b1[c], p[left, half_b(c), :])
                two(o, 1, c).start()

        @pl.when(s >= LE)
        def _():
            for o in range(2):
                c = s - LE + o * mh
                me = reduce_me[o]
                direct(o, 1, c).wait_recv()
                two(o, 0, c).wait_recv()
                out[half_a(c), :] = add(p[me, half_a(c), :], a2[c], dr[c])
                direct(o, 0, c).wait_recv()
                two(o, 1, c).wait_recv()
                out[half_b(c), :] = add(p[me, half_b(c), :], b2[c], dl[c])
                store_out(c).start()

        @pl.when(s == 0)
        def _():
            for k in range(4):
                gx(k).wait_recv()
                gwx[k] = add(gwx[k], gwt[2 * k + core])
            for k in range(4):
                gy(k).start()

        @pl.when(s == 4)
        def _():
            gy(0).wait_recv()
            ga1[...] = add(ga1[...], gwx[ys[0], A, :])
            gy(4).start()
            gy(1).wait_recv()
            gb1[...] = add(gb1[...], gwx[ys[1], B, :])
            gy(5).start()

        @pl.when(s == 8)
        def _():
            gy(3).wait_recv()
            gy(4).wait_recv()
            gwo[A, :] = add(gwx[y, A, :], ga2[...], gdr[...])
            gy(2).wait_recv()
            gy(5).wait_recv()
            gwo[B, :] = add(gwx[y, B, :], gb2[...], gdl[...])
            store_gw.start()

    for k in range(3):
        wz(k).wait_send()
        for j in range(4):
            wx(k, j).wait_send()
        for o in range(2):
            wy(o, k).wait_send()
    for k in range(4):
        gx(k).wait_send()
        for o in range(2):
            wc(o, k).wait_send()
    for k in range(6):
        gy(k).wait_send()

    @pl.loop(0, nh)
    def _(s):
        for o in range(2):
            for k in range(2):
                own(o, k, s + o * nh).wait_send()
                fwd(o, k, s + o * nh).wait_send()

    @pl.loop(0, mh)
    def _(s):
        for o in range(2):
            c = s + o * mh
            for k in range(2):
                hop(o, k, c).wait_send()
                direct(o, k, c).wait_send()
                two(o, k, c).wait_send()
            store_out(c).wait()

    store_gw.wait()


def local(hidden, weight, block_ids, targets):
    rows, width = hidden.shape
    owned = weight.shape[0]
    nb, nc = rows // RL, rows // RB
    dma = pltpu.SemaphoreType.DMA
    v = lambda *shape: pltpu.VMEM(shape, BF16)
    scratch = [
        v(rows, width), v(owned, width), v(2, 4, owned, 1024), v(4, rows, owned), v(owned, rows), v(4, rows, 256),
    ] + [v(nc, RB // 2, 256)] * 6 + [
        v(rows, 256), v(8, owned, 512), v(4, owned, 512),
    ] + [v(128, 512)] * 6 + [
        v(owned, 512),
        dma((nb,)), dma((6,)), dma((nc,)), dma((1,)),
        dma((3,)), dma((3,)), dma((3, 4)), dma((3, 4)), dma((2, 3)), dma((2, 3)), dma((2, 4)), dma((2, 4)),
    ] + [dma((2, nb))] * 4 + [dma((2, nc))] * 6 + [dma((4,)), dma((4,)), dma((6,)), dma((6,))]
    anywhere = pl.BlockSpec(memory_space=pl.ANY)
    return pl.pallas_call(
        kernel,
        out_shape=(jax.ShapeDtypeStruct((rows, 256), BF16), jax.ShapeDtypeStruct((owned, 512), BF16)),
        in_specs=[pl.BlockSpec(memory_space=pltpu.SMEM), pl.BlockSpec(memory_space=pltpu.VMEM), anywhere, anywhere],
        out_specs=(anywhere, anywhere),
        scratch_shapes=scratch,
        compiler_params=pltpu.CompilerParams(
            collective_id=0, has_side_effects=True, vmem_limit_bytes=60 * 1024 * 1024),
        cost_estimate=pl.CostEstimate(
            flops=6 * rows * owned * width, bytes_accessed=2 * rows * width, transcendentals=rows * owned),
    )(block_ids.T, targets.T, hidden, weight)


def solution(mesh):
    return jax.shard_map(
        local,
        mesh=mesh,
        in_specs=(P("dp", None), P("head", None), P("dp", None), P("dp", None)),
        out_specs=(P("dp", "head"), P("head", "dp")),
        check_vma=False,
    )
```

time: 257 us -> 79.8 us (0.31)
  waiting for transfers between devices: 179 us -> 0 us
  Pallas kernels: 0 us -> 75.6 us
  matrix products: 39.1 us -> 0 us
  other arithmetic: 19.2 us -> 0 us
  between operations: 14.1 us -> 0.65 us
    reduce_scatter x2 -> x0, waiting for transfers between devices: 179 us -> none  [the longest x1 156 us: local(): lax.psum_scatter(hidden_part.astype(jnp.bfloat16), 'head', scatter_dimens...]
    pallas_call x0 -> x1, Pallas kernels: none -> 75.6 us  [local(): pl.pallas_call(kernel, out_shape=(jax.ShapeDtypeStruct((rows, 256), BF16)...]
    dot_general x3 -> x0, matrix products: 39.1 us -> none  [the longest x1 13.3 us: local(): jnp.einsum('rl,rd->ld', grads, hidden, preferred_element_type=jnp.float32)]
    reduce_or x2 -> x0, other arithmetic: 19.1 us -> none  [the longest x1 18.2 us: local(): hits = jnp.any(targets[:, :, None] == labels[None, None, :], axis=1)]
  transfers between devices with their start and end apart: 2 -> 0, of which waited for: 2 -> 0; matrix products, arithmetic and copies ran while one was open for 5% -> 0% of each run, Pallas kernels for 0% -> 0%
where the time goes in v2:
time: 79.8 us; the launch traced here: 79.6 us
  Pallas kernels  75.6 us (95%)
  local copies, waits for them, and re-layouts  3.4 us (4%)
    pallas_call x1, Pallas kernels, local(): pl.pallas_call(kernel, out_shape=(jax.ShapeDtypeStruct((rows, 256), BF16)...  75.6 us
    unnamed x4, local copies, waits for them, and re-layouts  3.4 us

profile of v2, /device:TPU:0, one launch (start us, length us, event | category | flops | bytes accessed | tf_op | source)
XLA Modules:
  0.0 79.6 jit_solution(17547965790157676165)
XLA Ops:
  0.6 75.6 %shard_map.59 = (bf16[3072,256]{1,0:T(8,128)(2,1)}, bf16[256,512]{1,0:T(8,128)(2,1)}) custom-call(s32[8,12]{1,0:T(8,128)} %bitcast.3, s32[8,3072]{1,0:T(8,128)} %bitcast.2, bf16[3072,4096]{1,0:T(8,128)(2,1)} %hid_hbm.1, bf16[256,4096]{1,0:T(8,128)(2,1)} %w_hbm.1), custom_call_target="tpu_custom_call" | custom-call | flops 19327352832 | bytes 25165824 | tf_op jit(solution)/shard_map/pallas_call | solution.py:373
  76.2 0.0 copy-start
  76.2 2.7 %copy.8 = bf16[3072,256]{1,0:T(8,128)(2,1)} copy(bf16[3072,256]{1,0:T(8,128)(2,1)} %get-tuple-element.4) | data formatting | bytes 3145728
  78.9 0.0 copy-done
  78.9 0.7 copy.9
Async XLA Ops:
  76.2 2.7 %copy-start = (bf16[256,512]{1,0:T(8,128)(2,1)S(1)}, bf16[256,512]{1,0:T(8,128)(2,1)}, u32[]{:S(2)}) copy-start(bf16[256,512]{1,0:T(8,128)(2,1)} %get-tuple-element.5) | copy-start | bytes 786436

commit v3 on v2

--- a/solution.py
+++ b/solution.py
@@ -10,13 +10,13 @@
 F32 = jnp.float32
 BF16 = jnp.bfloat16
 RL = 256
-RB = 128
-
-
-def kernel(ids_ref, tgt_ref, hid_hbm, w_hbm, gh_hbm, gw_hbm,
-           hid, w, wq, g, gt, p, a1, b1, a2, b2, dl, dr, out,
-           gwt, gwx, ga1, gb1, ga2, gb2, gdl, gdr, gwo,
-           hid_sem, w_sem, out_sem, gwo_sem,
+RB = 256
+
+
+def kernel(ids_ref, tgt_ref, hid_hbm, w_hbm, out, gwo,
+           hid, w, wq, g, gt, p, a1, b1, a2, b2, dl, dr,
+           gwt, gwx, ga1, gb1, ga2, gb2, gdl, gdr,
+           hid_sem, w_sem,
            wz_s, wz_r, wx_s, wx_r, wy_s, wy_r, wc_s, wc_r,
            own_s, own_r, fwd_s, fwd_r, hop_s, hop_r, dir_s, dir_r, two_s, two_r,
            gx_s, gx_r, gy_s, gy_r):
@@ -78,11 +78,6 @@
     load_hid(0).start()
     load_hid(nb // 2).start()
 
-    @pl.loop(1, nb // 2)
-    def _(b):
-        load_hid(b).start()
-        load_hid(b + nb // 2).start()
-
     load_wz.start()
     for k in range(4):
         load_wx(k).start()
@@ -136,9 +131,6 @@
     def two(o, k, c):
         src, dst = ((a1, a2), (b1, b2))[k]
         return remote(src.at[c], dst.at[c], two_s.at[k, c], two_r.at[k, c], reduce_to[o][k])
-
-    def store_out(c):
-        return pltpu.make_async_copy(out.at[span(c * RB, RB)], gh_hbm.at[span(c * RB, RB)], out_sem.at[c])
 
     first = head * 2
     labels = first * BLOCK + lax.broadcasted_iota(jnp.int32, (2 * BLOCK, RL), 0)
@@ -178,8 +170,6 @@
             (ga1, ga2, 0), (gb1, gb2, 1))[k]
         return remote(src, dst, gy_s.at[k], gy_r.at[k], to_y[to])
 
-    store_gw = pltpu.make_async_copy(gwo, gw_hbm, gwo_sem.at[0])
-
     def add(*parts):
         total = parts[0].astype(F32)
         for part in parts[1:]:
@@ -189,7 +179,10 @@
     load_w.wait()
 
     nh = nb // 2
-    LA = 2
+    for o in range(2):
+        load_hid(o * nh + 1).start()
+
+    LA = 3
 
     @pl.loop(0, nh + 4)
     def _(s):
@@ -197,6 +190,11 @@
             @pl.when(s < nh)
             def _():
                 b = s + o * nh
+
+                @pl.when(s < nh - 2)
+                def _():
+                    load_hid(b + 2).start()
+
                 signal(b)
                 for k in range(2):
                     own(o, k, b).start()
@@ -252,11 +250,9 @@
     def _(s):
         @pl.when(s < mh)
         def _():
-            @pl.when(s % 2 == 0)
-            def _():
-                for o in range(2):
-                    for k in range(2):
-                        fwd(o, k, s // 2 + o * nh).wait_recv()
+            for o in range(2):
+                for k in range(2):
+                    fwd(o, k, s + o * nh).wait_recv()
 
             for o in range(2):
                 c = s + o * mh
@@ -292,7 +288,6 @@
                 direct(o, 0, c).wait_recv()
                 two(o, 1, c).wait_recv()
                 out[half_b(c), :] = add(p[me, half_b(c), :], b2[c], dl[c])
-                store_out(c).start()
 
         @pl.when(s == 0)
         def _():
@@ -302,7 +297,7 @@
             for k in range(4):
                 gy(k).start()
 
-        @pl.when(s == 4)
+        @pl.when(s == 2)
         def _():
             gy(0).wait_recv()
             ga1[...] = add(ga1[...], gwx[ys[0], A, :])
@@ -311,7 +306,7 @@
             gb1[...] = add(gb1[...], gwx[ys[1], B, :])
             gy(5).start()
 
-        @pl.when(s == 8)
+        @pl.when(s == 4)
         def _():
             gy(3).wait_recv()
             gy(4).wait_recv()
@@ -319,7 +314,6 @@
             gy(2).wait_recv()
             gy(5).wait_recv()
             gwo[B, :] = add(gwx[y, B, :], gb2[...], gdl[...])
-            store_gw.start()
 
     for k in range(3):
         wz(k).wait_send()
@@ -349,9 +343,6 @@
                 hop(o, k, c).wait_send()
                 direct(o, k, c).wait_send()
                 two(o, k, c).wait_send()
-            store_out(c).wait()
-
-    store_gw.wait()
 
 
 def local(hidden, weight, block_ids, targets):
@@ -363,21 +354,20 @@
     scratch = [
         v(rows, width), v(owned, width), v(2, 4, owned, 1024), v(4, rows, owned), v(owned, rows), v(4, rows, 256),
     ] + [v(nc, RB // 2, 256)] * 6 + [
-        v(rows, 256), v(8, owned, 512), v(4, owned, 512),
+        v(8, owned, 512), v(4, owned, 512),
     ] + [v(128, 512)] * 6 + [
-        v(owned, 512),
-        dma((nb,)), dma((6,)), dma((nc,)), dma((1,)),
+        dma((nb,)), dma((6,)),
         dma((3,)), dma((3,)), dma((3, 4)), dma((3, 4)), dma((2, 3)), dma((2, 3)), dma((2, 4)), dma((2, 4)),
     ] + [dma((2, nb))] * 4 + [dma((2, nc))] * 6 + [dma((4,)), dma((4,)), dma((6,)), dma((6,))]
     anywhere = pl.BlockSpec(memory_space=pl.ANY)
     return pl.pallas_call(
         kernel,
-        out_shape=(jax.ShapeDtypeStruct((rows, 256), BF16), jax.ShapeDtypeStruct((owned, 512), BF16)),
+        out_shape=(pltpu.VMEM((rows, 256), BF16), pltpu.VMEM((owned, 512), BF16)),
         in_specs=[pl.BlockSpec(memory_space=pltpu.SMEM), pl.BlockSpec(memory_space=pltpu.VMEM), anywhere, anywhere],
-        out_specs=(anywhere, anywhere),
+        out_specs=(pl.BlockSpec(memory_space=pltpu.VMEM),) * 2,
         scratch_shapes=scratch,
         compiler_params=pltpu.CompilerParams(
-            collective_id=0, has_side_effects=True, vmem_limit_bytes=60 * 1024 * 1024),
+            collective_id=0, has_side_effects=True, vmem_limit_bytes=57 * 1024 * 1024),
         cost_estimate=pl.CostEstimate(
             flops=6 * rows * owned * width, bytes_accessed=2 * rows * width, transcendentals=rows * owned),
     )(block_ids.T, targets.T, hidden, weight)

time: 79.8 us -> 71.7 us (0.90)
  Pallas kernels: 75.6 us -> 69 us
  local copies, waits for them, and re-layouts: 3.4 us -> 1.85 us
    pallas_call x1, Pallas kernels: 75.6 us -> 69 us  [local(): pl.pallas_call(kernel, out_shape=(pltpu.VMEM((rows, 256), BF16), pltpu.VM...]
    unnamed x4 -> x2, local copies, waits for them, and re-layouts: 3.4 us -> 1.85 us
where the time goes in v3:
time: 71.7 us; the launch traced here: 71.5 us
  Pallas kernels  69 us (96%)
  local copies, waits for them, and re-layouts  1.85 us (3%)
    pallas_call x1, Pallas kernels, local(): pl.pallas_call(kernel, out_shape=(pltpu.VMEM((rows, 256), BF16), pltpu.VM...  69 us
    unnamed x2, local copies, waits for them, and re-layouts  1.85 us

profile of v3, /device:TPU:0, one launch (start us, length us, event | category | flops | bytes accessed | tf_op | source)
XLA Modules:
  0.0 71.5 jit_solution(8950793787678773682)
XLA Ops:
  0.6 69.0 %shard_map.59 = (bf16[3072,256]{1,0:T(8,128)(2,1)S(1)}, bf16[256,512]{1,0:T(8,128)(2,1)S(1)}) custom-call(s32[8,12]{1,0:T(8,128)} %bitcast.3, s32[8,3072]{1,0:T(8,128)} %bitcast.2, bf16[3072,4096]{1,0:T(8,128)(2,1)} %hid_hbm.1, bf16[256,4096]{1,0:T(8,128)(2,1)} %w_hbm.1), custom_call_target="tpu_custom_call" | custom-call | flops 19327352832 | bytes 25165824 | tf_op jit(solution)/shard_map/pallas_call | solution.py:363
  69.7 1.1 %copy.8 = bf16[3072,256]{1,0:T(8,128)(2,1)} copy(bf16[3072,256]{1,0:T(8,128)(2,1)S(1)} %get-tuple-element.2) | data formatting | bytes 3145728
  70.8 0.7 copy.9

commit v4 on v3

--- a/solution.py
+++ b/solution.py
@@ -182,9 +182,9 @@
     for o in range(2):
         load_hid(o * nh + 1).start()
 
-    LA = 3
-
-    @pl.loop(0, nh + 4)
+    LA = 4
+
+    @pl.loop(0, nh + LA)
     def _(s):
         for o in range(2):
             @pl.when(s < nh)
@@ -220,18 +220,17 @@
                     wy(o, k).start()
                 wc(o, 0).start()
 
-        @pl.when(s == 7)
+        @pl.when(s == 8)
         def _():
             for o in range(2):
                 for k in range(3):
                     wy(o, k).wait_recv()
                     wc(o, k + 1).start()
 
-        @pl.when(s >= nh)
+        @pl.when((s >= nh) & (s < nh + 2))
         def _():
             for k in range(2):
-                i = 2 * (s - nh) + k
-                gw_tile(2 * lax.rem(i, 4) + jnp.where(i < 4, 1 - core, core))
+                gw_tile(2 * (2 * (s - nh) + k) + 1 - core)
 
         @pl.when((s >= nh) & (s < nh + 2))
         def _():
@@ -264,6 +263,10 @@
                     hop(o, k, c).start()
                 for k in range(2):
                     direct(o, k, c).start()
+
+        @pl.when(s < 4)
+        def _():
+            gw_tile(2 * s + core)
 
         @pl.when((s >= LD) & (s < mh + LD))
         def _():
@@ -289,7 +292,7 @@
                 two(o, 1, c).wait_recv()
                 out[half_b(c), :] = add(p[me, half_b(c), :], b2[c], dl[c])
 
-        @pl.when(s == 0)
+        @pl.when(s == 4)
         def _():
             for k in range(4):
                 gx(k).wait_recv()
@@ -297,7 +300,7 @@
             for k in range(4):
                 gy(k).start()
 
-        @pl.when(s == 2)
+        @pl.when(s == 6)
         def _():
             gy(0).wait_recv()
             ga1[...] = add(ga1[...], gwx[ys[0], A, :])
@@ -306,7 +309,7 @@
             gb1[...] = add(gb1[...], gwx[ys[1], B, :])
             gy(5).start()
 
-        @pl.when(s == 4)
+        @pl.when(s == 8)
         def _():
             gy(3).wait_recv()
             gy(4).wait_recv()

time: 71.7 us -> 68.7 us (0.958)
  Pallas kernels: 69 us -> 66 us
    pallas_call x1, Pallas kernels: 69 us -> 66 us  [local(): pl.pallas_call(kernel, out_shape=(pltpu.VMEM((rows, 256), BF16), pltpu.VM...]
where the time goes in v4:
time: 68.7 us; the launch traced here: 68.5 us
  Pallas kernels  66 us (96%)
  local copies, waits for them, and re-layouts  1.85 us (3%)
    pallas_call x1, Pallas kernels, local(): pl.pallas_call(kernel, out_shape=(pltpu.VMEM((rows, 256), BF16), pltpu.VM...  66 us
    unnamed x2, local copies, waits for them, and re-layouts  1.85 us

profile of v4, /device:TPU:0, one launch (start us, length us, event | category | flops | bytes accessed | tf_op | source)
XLA Modules:
  0.0 68.5 jit_solution(4368350958369230774)
XLA Ops:
  0.6 66.0 %shard_map.59 = (bf16[3072,256]{1,0:T(8,128)(2,1)S(1)}, bf16[256,512]{1,0:T(8,128)(2,1)S(1)}) custom-call(s32[8,12]{1,0:T(8,128)} %bitcast.3, s32[8,3072]{1,0:T(8,128)} %bitcast.2, bf16[3072,4096]{1,0:T(8,128)(2,1)} %hid_hbm.1, bf16[256,4096]{1,0:T(8,128)(2,1)} %w_hbm.1), custom_call_target="tpu_custom_call" | custom-call | flops 19327352832 | bytes 25165824 | tf_op jit(solution)/shard_map/pallas_call | solution.py:366
  66.7 1.1 %copy.8 = bf16[3072,256]{1,0:T(8,128)(2,1)} copy(bf16[3072,256]{1,0:T(8,128)(2,1)S(1)} %get-tuple-element.2) | data formatting | bytes 3145728
  67.8 0.7 %copy.9 = bf16[256,512]{1,0:T(8,128)(2,1)} copy(bf16[256,512]{1,0:T(8,128)(2,1)S(1)} %get-tuple-element.3) | data formatting | bytes 524288
